TPU v7x, 32 devices: a whole 2x2x4 slice. The times are simulated.
32 devices in a mesh: expert: 8 (over z, core), dp: 4 (over y, x).
Axes of the slice: x: 2, y: 2, z: 4, core: 2. Of those that a mesh axis runs over, the one named last changes fastest.
Arguments:
- tokens: bfloat16 [4096, 1024], P(('expert', 'dp')), may hold values from -6 to 6
- out_grad: bfloat16 [4096, 1024], P(('expert', 'dp')), may hold values from -0.59765625 to 0.59765625
- expert_ids: int32 [4096, 3], P(('expert', 'dp')), may hold values from 0 to 7, all different within a row; in each aligned block of 128 rows (0 to 127, 128 to 255, ...) at most 64 rows name the same one
- gate_probs: float32 [4096, 3], P(('expert', 'dp')), may hold values from 0.05 to 0.5
- w_gate: bfloat16 [8, 1024, 384], P('expert'), may hold values from -0.1875 to 0.1875
- w_up: bfloat16 [8, 1024, 384], P('expert'), may hold values from -0.1875 to 0.1875
- w_down: bfloat16 [8, 384, 1024], P('expert'), may hold values from -0.3125 to 0.3125
Outputs:
- grad_gate: bfloat16 [8, 1024, 384], P('expert', 'dp')
- grad_up: bfloat16 [8, 1024, 384], P('expert', 'dp')
- grad_down: bfloat16 [8, 384, 1024], P('expert', 'dp')
Inputs may be any that keep to these rules, and one draw needn't show every extreme that they name: `expert_ids`: each row names 3 different experts. In the 128 rows of one device no expert is named by more than 64 rows, a bound that some block reaches.
All inputs are finite; a program needn't handle non-finite values.
Results may differ from a plain program's by a relative error of at most 0.018.
Values may be sent and summed in bfloat16 or wider, within the bound.
A program may use at most 64 MiB of HBM per device.

v0:
```python
import jax
import jax.numpy as jnp
from jax import lax
from jax.sharding import PartitionSpec as P


def contract_rows(left, right):
    return lax.dot_general(
        left, right, (((0,), (0,)), ((), ())), preferred_element_type=jnp.float32
    )


def shards(tokens, out_grad, expert_ids, gate_probs, w_gate, w_up, w_down):
    experts = lax.axis_size("expert")
    tok_rows = tokens.shape[0]
    top_k = expert_ids.shape[1]
    width = tokens.shape[1]
    capacity = min(tok_rows, 4 * tok_rows * top_k // (3 * experts))
    columns = jnp.arange(experts, dtype=jnp.int32)
    hits = (expert_ids[:, :, None] == columns).astype(jnp.int32)
    token_hits = jnp.sum(hits, axis=1)
    before = jnp.cumsum(token_hits, axis=0) - token_hits
    rank = jnp.sum(hits * before[:, None, :], axis=2)
    scaled = (gate_probs[:, :, None] * out_grad[:, None, :].astype(jnp.float32)).astype(
        jnp.bfloat16
    )
    repeated = jnp.broadcast_to(tokens[:, None, :], scaled.shape)
    flat_slot = (expert_ids * capacity + rank).reshape(-1)
    send_in = (
        jnp.zeros((experts * capacity, width), jnp.bfloat16)
        .at[flat_slot]
        .set(repeated.reshape(-1, width))
    )
    send_grad = (
        jnp.zeros((experts * capacity, width), jnp.bfloat16)
        .at[flat_slot]
        .set(scaled.reshape(-1, width))
    )
    send_in = send_in.reshape(experts, capacity, width)
    send_grad = send_grad.reshape(experts, capacity, width)
    got_in, got_grad = (
        lax.all_to_all(send_in, "expert", split_axis=0, concat_axis=0, tiled=True),
        lax.all_to_all(send_grad, "expert", split_axis=0, concat_axis=0, tiled=True),
    )
    rows_in = got_in.reshape(-1, width)
    rows_grad = got_grad.reshape(-1, width)
    gate_pre = jnp.dot(rows_in, w_gate[0], preferred_element_type=jnp.float32)
    up_pre = jnp.dot(rows_in, w_up[0], preferred_element_type=jnp.float32)
    sigma = jax.nn.sigmoid(gate_pre)
    active = gate_pre * sigma
    hidden = (active * up_pre).astype(jnp.bfloat16)
    grad_down = contract_rows(hidden, rows_grad)
    grad_hidden = lax.dot_general(
        rows_grad, w_down[0], (((1,), (1,)), ((), ())), preferred_element_type=jnp.float32
    )
    grad_upper = (grad_hidden * active).astype(jnp.bfloat16)
    grad_gate_pre = (grad_hidden * up_pre * sigma * (1.0 + gate_pre * (1.0 - sigma))).astype(
        jnp.bfloat16
    )
    grad_gate = contract_rows(rows_in, grad_gate_pre)
    grad_up = contract_rows(rows_in, grad_upper)
    sum_gate, sum_up, sum_down = (
        lax.psum_scatter(
            grad_gate[None].astype(jnp.bfloat16), "dp", scatter_dimension=1, tiled=True
        ).astype(jnp.float32),
        lax.psum_scatter(
            grad_up[None].astype(jnp.bfloat16), "dp", scatter_dimension=1, tiled=True
        ).astype(jnp.float32),
        lax.psum_scatter(
            grad_down[None].astype(jnp.bfloat16), "dp", scatter_dimension=1, tiled=True
        ).astype(jnp.float32),
    )
    return (
        sum_gate.astype(jnp.bfloat16),
        sum_up.astype(jnp.bfloat16),
        sum_down.astype(jnp.bfloat16),
    )


def solution(mesh):
    return jax.shard_map(
        shards,
        mesh=mesh,
        in_specs=(
            P(("expert", "dp"), None),
            P(("expert", "dp"), None),
            P(("expert", "dp"), None),
            P(("expert", "dp"), None),
            P("expert", None, None),
            P("expert", None, None),
            P("expert", None, None),
        ),
        out_specs=(P("expert", "dp", None), P("expert", "dp", None), P("expert", "dp", None)),
        check_vma=False,
    )
```

profile of v0, /device:TPU:0, one launch (start us, length us, event | category | flops | bytes accessed | tf_op | source)
XLA Modules:
  0.0 173.8 jit_solution(15862193931348732459)
XLA Ops:
  7.2 0.0 copy-start
  7.2 0.8 convert_reduce_fusion
  7.9 0.1 copy.14
  8.0 0.2 reduce_window_sum.11
  8.3 0.7 select_reduce_fusion
  9.0 0.7 multiply_add_fusion
  9.7 0.1 copy.17
  9.8 0.2 reshape.73
  10.0 1.3 broadcast_in_dim.2
  11.3 0.7 reshape.83
  12.0 0.0 copy-start.5
  12.0 3.1 %scatter_custom_fusion = bf16[512,1024]{1,0:T(8,128)(2,1)} fusion(s32[384]{0:T(512)S(1)} %fusion.18, bf16[384,1024]{1,0:T(8,128)(2,1)S(1)} %reshape.83, bf16[]{:T(256)} %constant.5.clone.1), kind=kCustom, calls=%fused_computation.23 | custom fusion | bytes 1048578 | tf_op jit(solution)/shard_map/scatter | solution.py:32
  15.1 6.4 %all-to-all-start = ((bf16[8,64,1024]{2,1,0:T(8,128)(2,1)}), bf16[8,64,1024]{2,1,0:T(8,128)(2,1)S(1)}, u32[]{:S(2)}, u32[]{:S(2)}) async-start(bf16[8,64,1024]{2,1,0:T(8,128)(2,1)} %bitcast), calls=%async_computation | async-start | bytes 2097152 | tf_op jit(solution)/shard_map/all_to_all | solution.py:42
  21.5 0.0 copy-done.5
  21.5 1.9 %mul.59 = f32[128,3,1024]{2,1,0:T(4,128)} broadcast(bf16[128,1024]{1,0:T(8,128)(2,1)S(1)} %copy-done.5), dimensions={0,2} | broadcast | bytes 1835008 | tf_op jit(solution)/shard_map/mul | solution.py:24
  23.4 0.0 copy-start.6
  23.4 2.7 %mul.60 = f32[384,1024]{1,0:T(8,128)S(1)} reshape(f32[128,3,1024]{2,1,0:T(4,128)} %mul.59) | data formatting | bytes 3145728 | tf_op jit(solution)/shard_map/mul | solution.py:24
  26.1 0.0 copy-done.6
  26.1 0.1 copy.18
  26.2 0.2 mul.57
  26.5 3.1 %scatter_custom_fusion.1 = bf16[512,1024]{1,0:T(8,128)(2,1)} fusion(s32[384]{0:T(512)S(1)} %fusion.18, f32[384,1024]{1,0:T(8,128)S(1)} %mul.60, f32[384]{0:T(512)S(1)} %mul.57, bf16[]{:T(256)} %constant.5.clone.1), kind=kCustom, calls=%fused_computation.9 | custom fusion | flops 786432 | bytes 2623490 | tf_op jit(solution)/shard_map/scatter | solution.py:37
  29.6 18.4 %all-to-all-done = bf16[8,64,1024]{2,1,0:T(8,128)(2,1)S(1)} async-done(((bf16[8,64,1024]{2,1,0:T(8,128)(2,1)}), bf16[8,64,1024]{2,1,0:T(8,128)(2,1)S(1)}, u32[]{:S(2)}, u32[]{:S(2)}) %all-to-all-start) | async-done | bytes 1048608 | tf_op jit(solution)/shard_map/all_to_all | solution.py:42
  48.0 3.6 %all-to-all-start.1 = ((bf16[8,64,1024]{2,1,0:T(8,128)(2,1)}), bf16[8,64,1024]{2,1,0:T(8,128)(2,1)S(1)}, u32[]{:S(2)}, u32[]{:S(2)}) async-start(bf16[8,64,1024]{2,1,0:T(8,128)(2,1)} %bitcast.31), calls=%async_computation.1 | async-start | bytes 2097152 | tf_op jit(solution)/shard_map/all_to_all | solution.py:43
  51.6 0.0 reduce-scatter.4.cloned.1.call-start
  51.7 0.0 copy-start.1
  51.7 0.0 copy-done
  51.7 1.6 fusion.4
  53.3 0.0 copy-done.1
  53.3 1.6 fusion.6
  54.9 23.2 %all-to-all-done.1 = bf16[8,64,1024]{2,1,0:T(8,128)(2,1)S(1)} async-done(((bf16[8,64,1024]{2,1,0:T(8,128)(2,1)}), bf16[8,64,1024]{2,1,0:T(8,128)(2,1)S(1)}, u32[]{:S(2)}, u32[]{:S(2)}) %all-to-all-start.1) | async-done | bytes 1048608 | tf_op jit(solution)/shard_map/all_to_all | solution.py:43
  78.1 0.0 copy-start.2
  78.1 0.0 copy-start.3
  78.1 2.0 %fusion.8 = f32[512,384]{1,0:T(8,128)S(1)} fusion(bf16[512,1024]{1,0:T(8,128)(2,1)S(1)} %bitcast.29, bf16[1,384,1024]{2,1,0:T(8,128)(2,1)} %param.13), kind=kOutput, calls=%fused_computation.14 | convolution fusion | flops 402653184 | bytes 2621440 | tf_op jit(solution)/shard_map/dot_general | solution.py:53
  80.1 0.0 copy-start.4
  80.1 0.9 copy-done.4
  81.0 0.0 copy-done.2
  81.0 0.0 copy-done.3
  81.0 1.8 %fusion = bf16[1,1024,384]{2,1,0:T(8,128)(2,1)} fusion(bf16[512,1024]{1,0:T(8,128)(2,1)S(1)} %bitcast.27, f32[512,384]{1,0:T(8,128)S(1)} %copy-done.2, f32[512,384]{1,0:T(8,128)S(1)} %fusion.8, f32[512,384]{1,0:T(8,128)S(1)} %copy-done.3), kind=kOutput, calls=%fused_computation.6 | convolution fusion | flops 405012480 | bytes 4194304 | tf_op jit(solution)/shard_map/dot_general | solution.py:8
  82.7 0.0 reduce-scatter.4.cloned.1.call-update
  82.8 0.0 reduce-scatter.6.cloned.1.call-start
  82.8 3.1 %fusion.1 = bf16[1,1024,384]{2,1,0:T(8,128)(2,1)} fusion(bf16[512,1024]{1,0:T(8,128)(2,1)S(1)} %bitcast.28, f32[512,384]{1,0:T(8,128)} %copy-done.4, f32[512,384]{1,0:T(8,128)} %fusion.4), kind=kOutput, calls=%fused_computation.7 | convolution fusion | flops 404226048 | bytes 3407872 | tf_op jit(solution)/shard_map/dot_general | solution.py:8
  85.9 0.0 reduce-scatter.6.cloned.1.call-update
  85.9 0.0 reduce-scatter.8.cloned.1.call-start
  86.0 2.9 %fusion.2 = bf16[1,384,1024]{2,1,0:T(8,128)(2,1)} fusion(bf16[512,1024]{1,0:T(8,128)(2,1)S(1)} %bitcast.30, f32[512,384]{1,0:T(8,128)} %fusion.6, f32[512,384]{1,0:T(8,128)} %fusion.4), kind=kOutput, calls=%fused_computation.8 | convolution fusion | flops 404226048 | bytes 3407872 | tf_op jit(solution)/shard_map/dot_general | solution.py:8
  88.9 0.0 reduce-scatter.8.cloned.1.call-update
  88.9 19.1 %reduce-scatter.4.cloned.1.call-done = bf16[1,256,384]{2,1,0:T(8,128)(2,1)} async-done(((bf16[1,1024,384]{2,1,0:T(8,128)(2,1)}), bf16[1,256,384]{2,1,0:T(8,128)(2,1)}) %reduce-scatter.4.cloned.1.call-update) | async-done | bytes 196624 | tf_op jit(solution)/shard_map/reduce_scatter | solution.py:63
  108.0 29.7 %reduce-scatter.6.cloned.1.call-done = bf16[1,256,384]{2,1,0:T(8,128)(2,1)} async-done(((bf16[1,1024,384]{2,1,0:T(8,128)(2,1)}), bf16[1,256,384]{2,1,0:T(8,128)(2,1)}) %reduce-scatter.6.cloned.1.call-update) | async-done | bytes 196624 | tf_op jit(solution)/shard_map/reduce_scatter | solution.py:66
  137.6 29.7 %reduce-scatter.8.cloned.1.call-done = bf16[1,96,1024]{2,1,0:T(8,128)(2,1)} async-done(((bf16[1,384,1024]{2,1,0:T(8,128)(2,1)}), bf16[1,96,1024]{2,1,0:T(8,128)(2,1)}) %reduce-scatter.8.cloned.1.call-update) | async-done | bytes 196624 | tf_op jit(solution)/shard_map/reduce_scatter | solution.py:69
  (3 shorter events, 0.1 us)
Async XLA Ops:
  7.2 44.5 %copy-start = (bf16[1,1024,384]{2,1,0:T(8,128)(2,1)S(1)}, bf16[1,1024,384]{2,1,0:T(8,128)(2,1)}, u32[]{:S(2)}) copy-start(bf16[1,1024,384]{2,1,0:T(8,128)(2,1)} %param.11) | copy-start | bytes 2359300
  12.0 9.5 %copy-start.5 = (bf16[128,1024]{1,0:T(8,128)(2,1)S(1)}, bf16[128,1024]{1,0:T(8,128)(2,1)}, u32[]{:S(2)}) copy-start(bf16[128,1024]{1,0:T(8,128)(2,1)} %param.8) | copy-start | bytes 786436
  15.1 32.9 %all-to-all-start = ((bf16[8,64,1024]{2,1,0:T(8,128)(2,1)}), bf16[8,64,1024]{2,1,0:T(8,128)(2,1)S(1)}, u32[]{:S(2)}, u32[]{:S(2)}) async-start(bf16[8,64,1024]{2,1,0:T(8,128)(2,1)} %bitcast), calls=%async_computation | async-start | bytes 2097152 | tf_op jit(solution)/shard_map/all_to_all | solution.py:42
  23.4 2.7 %copy-start.6 = (f32[128,3]{0,1:T(4,128)S(1)}, f32[128,3]{0,1:T(4,128)}, u32[]{:S(2)}) copy-start(f32[128,3]{0,1:T(4,128)} %param.10) | copy-start | bytes 4612
  48.0 30.1 %all-to-all-start.1 = ((bf16[8,64,1024]{2,1,0:T(8,128)(2,1)}), bf16[8,64,1024]{2,1,0:T(8,128)(2,1)S(1)}, u32[]{:S(2)}, u32[]{:S(2)}) async-start(bf16[8,64,1024]{2,1,0:T(8,128)(2,1)} %bitcast.31), calls=%async_computation.1 | async-start | bytes 2097152 | tf_op jit(solution)/shard_map/all_to_all | solution.py:43
  51.6 56.4 %reduce-scatter.4.cloned.1.call-start = ((), (), s32[]{:S(2)}) async-start(), calls=%async_computation.5 | async-start | bytes 983040 | tf_op jit(solution)/shard_map/reduce_scatter | solution.py:63
  51.7 1.6 copy-start.1
  78.1 2.9 %copy-start.2 = (f32[512,384]{1,0:T(8,128)S(1)}, f32[512,384]{1,0:T(8,128)}, u32[]{:S(2)}) copy-start(f32[512,384]{1,0:T(8,128)} %fusion.4) | copy-start | bytes 2359300
  78.1 2.9 %copy-start.3 = (f32[512,384]{1,0:T(8,128)S(1)}, f32[512,384]{1,0:T(8,128)}, u32[]{:S(2)}) copy-start(f32[512,384]{1,0:T(8,128)} %fusion.6) | copy-start | bytes 2359300
  80.1 0.9 copy-start.4
  82.8 54.9 %reduce-scatter.6.cloned.1.call-start = ((), (), s32[]{:S(2)}) async-start(), calls=%async_computation.6 | async-start | bytes 983040 | tf_op jit(solution)/shard_map/reduce_scatter | solution.py:66
  85.9 81.4 %reduce-scatter.8.cloned.1.call-start = ((), (), s32[]{:S(2)}) async-start(), calls=%async_computation.7 | async-start | bytes 983040 | tf_op jit(solution)/shard_map/reduce_scatter | solution.py:69
Sparse Core Ops, SparseCore 0:
  82.9 25.0 reduce-scatter.3
  111.5 26.1 reduce-scatter.5
  141.1 26.1 reduce-scatter.7
where the time goes:
time: 174 us
  waiting for transfers between devices  120 us (69%)
  between operations  13.8 us (8%)
  matrix products  12.9 us (7%)
  local copies, waits for them, and re-layouts  11.4 us (7%)
  starting transfers between devices  10 us (6%)
  other arithmetic  5.52 us (3%)
    reduce_scatter x1, waiting for transfers between devices, shards(): lax.psum_scatter(grad_down[None].astype(jnp.bfloat16), 'dp', scatter_dime...  29.7 us
    reduce_scatter x1, waiting for transfers between devices, shards(): lax.psum_scatter(grad_up[None].astype(jnp.bfloat16), 'dp', scatter_dimens...  29.7 us
    all_to_all x1, waiting for transfers between devices, shards(): lax.all_to_all(send_grad, 'expert', split_axis=0, concat_axis=0, tiled=True)  23.2 us
    reduce_scatter x1, waiting for transfers between devices, shards(): lax.psum_scatter(grad_gate[None].astype(jnp.bfloat16), 'dp', scatter_dime...  19.1 us
    all_to_all x1, waiting for transfers between devices, shards(): lax.all_to_all(send_in, 'expert', split_axis=0, concat_axis=0, tiled=True)  18.4 us
    dot_general x3, matrix products, contract_rows(): lax.dot_general(left, right, (((0,), (0,)), ((), ())), preferred_element_...  7.74 us
    all_to_all x1, starting transfers between devices, shards(): lax.all_to_all(send_in, 'expert', split_axis=0, concat_axis=0, tiled=True)  6.35 us
    mul x3, local copies, waits for them, and re-layouts, shards(): gate_probs[:, :, None] * out_grad[:, None, :].astype(jnp.float32)  4.83 us
  transfers between devices with their start and end apart: 5, of which 5 were waited for; matrix products, arithmetic and copies ran while one was open for 10% of the time, Pallas kernels for 0%

commit v1 on v0

--- a/solution.py
+++ b/solution.py
@@ -2,6 +2,22 @@
 import jax.numpy as jnp
 from jax import lax
 from jax.sharding import PartitionSpec as P
+
+
+def exchange_in_pairs(x, axis, split, join):
+    ways, here = (lax.axis_size(axis), lax.axis_index(axis))
+    width = x.shape[split] // ways
+    lengths = list(x.shape)
+    lengths[split] = width
+    height = lengths[join]
+    lengths[join] = height * ways
+    full = jnp.zeros(lengths, x.dtype)
+    for mask in range(ways):
+        part = lax.dynamic_slice_in_dim(x, (here ^ mask) * width, width, axis=split)
+        if mask:
+            part = lax.ppermute(part, axis, [(d, d ^ mask) for d in range(ways)])
+        full = lax.dynamic_update_slice_in_dim(full, part, (here ^ mask) * height, axis=join)
+    return full
 
 
 def contract_rows(left, right):
@@ -40,7 +56,7 @@
     send_grad = send_grad.reshape(experts, capacity, width)
     got_in, got_grad = (
         lax.all_to_all(send_in, "expert", split_axis=0, concat_axis=0, tiled=True),
-        lax.all_to_all(send_grad, "expert", split_axis=0, concat_axis=0, tiled=True),
+        exchange_in_pairs(send_grad, "expert", 0, 0),
     )
     rows_in = got_in.reshape(-1, width)
     rows_grad = got_grad.reshape(-1, width)

time: 174 us -> 165 us (0.948)
  waiting for transfers between devices: 120 us -> 105 us
  starting transfers between devices: 10 us -> 17.2 us
  matrix products: 12.9 us -> 9.46 us
  local copies, waits for them, and re-layouts: 11.4 us -> 14 us
    all_to_all x1 -> x0, waiting for transfers between devices: 23.2 us -> none  [shards(): lax.all_to_all(send_grad, 'expert', split_axis=0, concat_axis=0, tiled=True)]
    ppermute x0 -> x7, waiting for transfers between devices: none -> 22.5 us  [exchange_in_pairs(): part = lax.ppermute(part, axis, [(d, d ^ mask) for d in range(ways)])]
    all_to_all x1, waiting for transfers between devices: 18.4 us -> 0.01 us  [shards(): lax.all_to_all(send_in, 'expert', split_axis=0, concat_axis=0, tiled=True)]
    ppermute x0 -> x7, starting transfers between devices: none -> 10.8 us  [exchange_in_pairs(): part = lax.ppermute(part, axis, [(d, d ^ mask) for d in range(ways)])]
    reduce_scatter x1, waiting for transfers between devices: 19.1 us -> 29.6 us  [shards(): lax.psum_scatter(grad_gate[None].astype(jnp.bfloat16), 'dp', scatter_dime...]
    reduce_scatter x1, waiting for transfers between devices: 29.7 us -> 22.9 us  [shards(): lax.psum_scatter(grad_down[None].astype(jnp.bfloat16), 'dp', scatter_dime...]
    all_to_all x1 -> x0, starting transfers between devices: 3.56 us -> none  [shards(): lax.all_to_all(send_grad, 'expert', split_axis=0, concat_axis=0, tiled=True)]
    unnamed x15 -> x23, local copies, waits for them, and re-layouts: 1.02 us -> 3.39 us
  transfers between devices with their start and end apart: 5 -> 11, of which waited for: 5 -> 7; matrix products, arithmetic and copies ran while one was open for 10% -> 9% of each run, Pallas kernels for 0% -> 0%
where the time goes in v1:
time: 165 us
  waiting for transfers between devices  105 us (64%)
  starting transfers between devices  17.2 us (10%)
  local copies, waits for them, and re-layouts  14 us (8%)
  between operations  14 us (8%)
  matrix products  9.46 us (6%)
  other arithmetic  5.53 us (3%)
    reduce_scatter x1, waiting for transfers between devices, shards(): lax.psum_scatter(grad_up[None].astype(jnp.bfloat16), 'dp', scatter_dimens...  29.7 us
    reduce_scatter x1, waiting for transfers between devices, shards(): lax.psum_scatter(grad_gate[None].astype(jnp.bfloat16), 'dp', scatter_dime...  29.6 us
    reduce_scatter x1, waiting for transfers between devices, shards(): lax.psum_scatter(grad_down[None].astype(jnp.bfloat16), 'dp', scatter_dime...  22.9 us
    ppermute x7, waiting for transfers between devices, exchange_in_pairs(): part = lax.ppermute(part, axis, [(d, d ^ mask) for d in range(ways)])  22.5 us
    ppermute x7, starting transfers between devices, exchange_in_pairs(): part = lax.ppermute(part, axis, [(d, d ^ mask) for d in range(ways)])  10.8 us
    all_to_all x1, starting transfers between devices, shards(): lax.all_to_all(send_in, 'expert', split_axis=0, concat_axis=0, tiled=True)  6.35 us
    dot_general x3, matrix products, contract_rows(): lax.dot_general(left, right, (((0,), (0,)), ((), ())), preferred_element_...  6.11 us
    mul x3, local copies, waits for them, and re-layouts, shards(): gate_probs[:, :, None] * out_grad[:, None, :].astype(jnp.float32)  4.82 us
  transfers between devices with their start and end apart: 11, of which 7 were waited for; matrix products, arithmetic and copies ran while one was open for 9% of the time, Pallas kernels for 0%

profile of v1, /device:TPU:0, one launch (start us, length us, event | category | flops | bytes accessed | tf_op | source)
XLA Modules:
  0.0 165.0 jit_solution(293870779955969632)
XLA Ops:
  7.2 0.0 copy-start
  7.2 0.8 convert_reduce_fusion
  7.9 0.1 copy.14
  8.0 0.2 reduce_window_sum.11
  8.3 0.7 select_reduce_fusion
  9.0 0.7 multiply_add_fusion
  9.7 0.1 copy.17
  9.8 0.2 reshape.73
  10.0 1.3 broadcast_in_dim.4
  11.3 0.7 reshape.83
  12.0 0.0 copy-start.9
  12.0 3.1 %scatter_custom_fusion = bf16[512,1024]{1,0:T(8,128)(2,1)} fusion(s32[384]{0:T(512)S(1)} %fusion.18, bf16[384,1024]{1,0:T(8,128)(2,1)S(1)} %reshape.83, bf16[]{:T(256)} %constant.15.clone.1), kind=kCustom, calls=%fused_computation.23 | custom fusion | bytes 1048578 | tf_op jit(solution)/shard_map/scatter | solution.py:48
  15.1 6.4 %all-to-all-start = ((bf16[8,64,1024]{2,1,0:T(8,128)(2,1)}), bf16[8,64,1024]{2,1,0:T(8,128)(2,1)S(1)}, u32[]{:S(2)}, u32[]{:S(2)}) async-start(bf16[8,64,1024]{2,1,0:T(8,128)(2,1)} %bitcast), calls=%async_computation | async-start | bytes 2097152 | tf_op jit(solution)/shard_map/all_to_all | solution.py:58
  21.5 0.0 reduce-scatter.8.cloned.1.call-start
  21.6 0.0 copy-done.9
  21.6 1.9 %mul.59 = f32[128,3,1024]{2,1,0:T(4,128)} broadcast(bf16[128,1024]{1,0:T(8,128)(2,1)S(1)} %copy-done.9), dimensions={0,2} | broadcast | bytes 1835008 | tf_op jit(solution)/shard_map/mul | solution.py:40
  23.5 2.7 %mul.60 = f32[384,1024]{1,0:T(8,128)S(1)} reshape(f32[128,3,1024]{2,1,0:T(4,128)} %mul.59) | data formatting | bytes 3145728 | tf_op jit(solution)/shard_map/mul | solution.py:40
  26.2 0.0 copy-done.10
  26.2 0.1 copy.18
  26.3 0.2 mul.57
  26.6 3.2 %scatter_custom_fusion.1 = bf16[512,1024]{1,0:T(8,128)(2,1)} fusion(s32[384]{0:T(512)S(1)} %fusion.18, f32[384,1024]{1,0:T(8,128)S(1)} %mul.60, f32[384]{0:T(512)S(1)} %mul.57, bf16[]{:T(256)} %constant.15.clone.1), kind=kCustom, calls=%fused_computation.9 | custom fusion | flops 786432 | bytes 2623490 | tf_op jit(solution)/shard_map/scatter | solution.py:53
  29.7 0.1 broadcast_in_dim.5
  29.8 1.1 copy-done.1
  30.9 0.1 constant_dynamic-slice_fusion
  31.0 0.5 collective-permute-start
  31.5 1.6 collective-permute-start.1
  33.2 0.0 collective-permute-start.2
  33.2 2.6 %collective-permute-start.3 = (bf16[1,64,1024]{2,1,0:T(8,128)(2,1)S(1)}, bf16[1,64,1024]{2,1,0:T(8,128)(2,1)S(1)}, u32[]{:S(2)}, u32[]{:S(2)}) collective-permute-start(bf16[1,64,1024]{2,1,0:T(8,128)(2,1)S(1)} %get-tuple-element.6), channel_id=1, source_target_pairs={{0,16},{4,20},{8,24},{12,28},{16,0},{20,4},{24,8},{28,12},{1,17},{... | collective-permute-start | bytes 393224 | tf_op jit(solution)/shard_map/ppermute | solution.py:18
  35.8 0.1 collective-permute-start.4
  35.9 0.0 collective-permute-done
  35.9 3.4 %collective-permute-start.5 = (bf16[1,64,1024]{2,1,0:T(8,128)(2,1)S(1)}, bf16[1,64,1024]{2,1,0:T(8,128)(2,1)S(1)}, u32[]{:S(2)}, u32[]{:S(2)}) collective-permute-start(bf16[1,64,1024]{2,1,0:T(8,128)(2,1)S(1)} %get-tuple-element.4), channel_id=1, source_target_pairs={{0,24},{4,28},{8,16},{12,20},{16,8},{20,12},{24,0},{28,4},{1,25},{... | collective-permute-start | bytes 393224 | tf_op jit(solution)/shard_map/ppermute | solution.py:18
  39.4 3.1 %collective-permute-done.1 = bf16[1,64,1024]{2,1,0:T(8,128)(2,1)S(1)} collective-permute-done((bf16[1,64,1024]{2,1,0:T(8,128)(2,1)S(1)}, bf16[1,64,1024]{2,1,0:T(8,128)(2,1)S(1)}, u32[]{:S(2)}, u32[]{:S(2)}) %collective-permute-start.1) | collective-permute-done | bytes 131104 | tf_op jit(solution)/shard_map/ppermute | solution.py:18
  42.5 2.4 %collective-permute-start.6 = (bf16[1,64,1024]{2,1,0:T(8,128)(2,1)S(1)}, bf16[1,64,1024]{2,1,0:T(8,128)(2,1)S(1)}, u32[]{:S(2)}, u32[]{:S(2)}) collective-permute-start(bf16[1,64,1024]{2,1,0:T(8,128)(2,1)S(1)} %get-tuple-element.3), channel_id=1, source_target_pairs={{0,28},{4,24},{8,20},{12,16},{16,12},{20,8},{24,4},{28,0},{1,29},{... | collective-permute-start | bytes 393224 | tf_op jit(solution)/shard_map/ppermute | solution.py:18
  44.9 0.3 collective-permute-done.2
  45.3 17.4 %collective-permute-done.3 = bf16[1,64,1024]{2,1,0:T(8,128)(2,1)S(1)} collective-permute-done((bf16[1,64,1024]{2,1,0:T(8,128)(2,1)S(1)}, bf16[1,64,1024]{2,1,0:T(8,128)(2,1)S(1)}, u32[]{:S(2)}, u32[]{:S(2)}) %collective-permute-start.3) | collective-permute-done | bytes 131104 | tf_op jit(solution)/shard_map/ppermute | solution.py:18
  62.7 1.6 collective-permute-done.4
  64.3 0.0 collective-permute-done.5
  64.4 0.0 collective-permute-done.6
  64.4 0.0 all-to-all-done
  64.4 0.0 copy-start.2
  64.4 0.0 copy-done
  64.4 0.7 fusion.4
  65.1 0.4 copy-done.2
  65.6 0.7 fusion.6
  66.3 0.0 copy-start.6
  66.3 0.2 copy-done.3
  66.4 0.7 copy-done.6
  67.1 1.5 fusion.2
  68.7 0.0 reduce-scatter.8.cloned.1.call-update
  68.7 0.0 reduce-scatter.6.cloned.1.call-start
  68.7 0.0 copy-start.4
  68.8 1.9 %fusion.8 = f32[512,384]{1,0:T(8,128)S(1)} fusion(bf16[512,1024]{1,0:T(8,128)(2,1)S(1)} %bitcast.31, bf16[1,384,1024]{2,1,0:T(8,128)(2,1)} %param.13), kind=kOutput, calls=%fused_computation.14 | convolution fusion | flops 402653184 | bytes 2621440 | tf_op jit(solution)/shard_map/dot_general | solution.py:69
  70.7 0.0 copy-start.8
  70.7 0.9 copy-done.8
  71.6 0.0 copy-done.4
  71.6 1.7 %fusion.1 = bf16[1,1024,384]{2,1,0:T(8,128)(2,1)} fusion(bf16[512,1024]{1,0:T(8,128)(2,1)S(1)} %bitcast.27, f32[512,384]{1,0:T(8,128)S(1)} %fusion.8, f32[512,384]{1,0:T(8,128)S(1)} %copy-done.4), kind=kOutput, calls=%fused_computation.7 | convolution fusion | flops 404226048 | bytes 3407872 | tf_op jit(solution)/shard_map/dot_general | solution.py:24
  73.3 0.0 reduce-scatter.6.cloned.1.call-update
  73.3 0.0 reduce-scatter.4.cloned.1.call-start
  73.4 0.0 copy-done.5
  73.4 2.9 %fusion = bf16[1,1024,384]{2,1,0:T(8,128)(2,1)} fusion(bf16[512,1024]{1,0:T(8,128)(2,1)S(1)} %bitcast.28, f32[512,384]{1,0:T(8,128)S(1)} %copy-done.5, f32[512,384]{1,0:T(8,128)} %copy-done.8, f32[512,384]{1,0:T(8,128)S(1)} %copy-done.7), kind=kOutput, calls=%fused_computation.6 | convolution fusion | flops 405012480 | bytes 4194304 | tf_op jit(solution)/shard_map/dot_general | solution.py:24
  76.3 0.0 reduce-scatter.4.cloned.1.call-update
  76.3 22.9 %reduce-scatter.8.cloned.1.call-done = bf16[1,96,1024]{2,1,0:T(8,128)(2,1)} async-done(((bf16[1,384,1024]{2,1,0:T(8,128)(2,1)}), bf16[1,96,1024]{2,1,0:T(8,128)(2,1)}) %reduce-scatter.8.cloned.1.call-update) | async-done | bytes 196624 | tf_op jit(solution)/shard_map/reduce_scatter | solution.py:85
  99.2 29.7 %reduce-scatter.6.cloned.1.call-done = bf16[1,256,384]{2,1,0:T(8,128)(2,1)} async-done(((bf16[1,1024,384]{2,1,0:T(8,128)(2,1)}), bf16[1,256,384]{2,1,0:T(8,128)(2,1)}) %reduce-scatter.6.cloned.1.call-update) | async-done | bytes 196624 | tf_op jit(solution)/shard_map/reduce_scatter | solution.py:82
  128.8 29.6 %reduce-scatter.4.cloned.1.call-done = bf16[1,256,384]{2,1,0:T(8,128)(2,1)} async-done(((bf16[1,1024,384]{2,1,0:T(8,128)(2,1)}), bf16[1,256,384]{2,1,0:T(8,128)(2,1)}) %reduce-scatter.4.cloned.1.call-update) | async-done | bytes 196624 | tf_op jit(solution)/shard_map/reduce_scatter | solution.py:79
  (16 shorter events, 0.2 us)
Async XLA Ops:
  7.2 57.3 %copy-start = (bf16[1,1024,384]{2,1,0:T(8,128)(2,1)S(1)}, bf16[1,1024,384]{2,1,0:T(8,128)(2,1)}, u32[]{:S(2)}) copy-start(bf16[1,1024,384]{2,1,0:T(8,128)(2,1)} %param.11) | copy-start | bytes 2359300
  12.0 9.6 %copy-start.9 = (bf16[128,1024]{1,0:T(8,128)(2,1)S(1)}, bf16[128,1024]{1,0:T(8,128)(2,1)}, u32[]{:S(2)}) copy-start(bf16[128,1024]{1,0:T(8,128)(2,1)} %param.8) | copy-start | bytes 786436
  15.1 49.3 %all-to-all-start = ((bf16[8,64,1024]{2,1,0:T(8,128)(2,1)}), bf16[8,64,1024]{2,1,0:T(8,128)(2,1)S(1)}, u32[]{:S(2)}, u32[]{:S(2)}) async-start(bf16[8,64,1024]{2,1,0:T(8,128)(2,1)} %bitcast), calls=%async_computation | async-start | bytes 2097152 | tf_op jit(solution)/shard_map/all_to_all | solution.py:58
  21.5 77.7 %reduce-scatter.8.cloned.1.call-start = ((), (), s32[]{:S(2)}) async-start(), calls=%async_computation.6 | async-start | bytes 983040 | tf_op jit(solution)/shard_map/reduce_scatter | solution.py:85
  23.5 2.7 %copy-start.10 = (f32[128,3]{0,1:T(4,128)S(1)}, f32[128,3]{0,1:T(4,128)}, u32[]{:S(2)}) copy-start(f32[128,3]{0,1:T(4,128)} %param.10) | copy-start | bytes 4612
  29.7 1.2 copy-start.1
  31.0 4.9 %collective-permute-start = (bf16[1,64,1024]{2,1,0:T(8,128)(2,1)S(1)}, bf16[1,64,1024]{2,1,0:T(8,128)(2,1)S(1)}, u32[]{:S(2)}, u32[]{:S(2)}) collective-permute-start(bf16[1,64,1024]{2,1,0:T(8,128)(2,1)S(1)} %get-tuple-element.9), channel_id=1, source_target_pairs={{0,4},{4,0},{8,12},{12,8},{16,20},{20,16},{24,28},{28,24},{1,5},{5... | collective-permute-start | bytes 393224 | tf_op jit(solution)/shard_map/ppermute | solution.py:18
  31.5 10.9 %collective-permute-start.1 = (bf16[1,64,1024]{2,1,0:T(8,128)(2,1)S(1)}, bf16[1,64,1024]{2,1,0:T(8,128)(2,1)S(1)}, u32[]{:S(2)}, u32[]{:S(2)}) collective-permute-start(bf16[1,64,1024]{2,1,0:T(8,128)(2,1)S(1)} %get-tuple-element.8), channel_id=1, source_target_pairs={{0,8},{4,12},{8,0},{12,4},{16,24},{20,28},{24,16},{28,20},{1,9},{5... | collective-permute-start | bytes 393224 | tf_op jit(solution)/shard_map/ppermute | solution.py:18
  33.2 12.1 %collective-permute-start.2 = (bf16[1,64,1024]{2,1,0:T(8,128)(2,1)S(1)}, bf16[1,64,1024]{2,1,0:T(8,128)(2,1)S(1)}, u32[]{:S(2)}, u32[]{:S(2)}) collective-permute-start(bf16[1,64,1024]{2,1,0:T(8,128)(2,1)S(1)} %get-tuple-element.7), channel_id=1, source_target_pairs={{0,12},{4,8},{8,4},{12,0},{16,28},{20,24},{24,20},{28,16},{1,13},{... | collective-permute-start | bytes 393224 | tf_op jit(solution)/shard_map/ppermute | solution.py:18
  33.2 29.5 %collective-permute-start.3 = (bf16[1,64,1024]{2,1,0:T(8,128)(2,1)S(1)}, bf16[1,64,1024]{2,1,0:T(8,128)(2,1)S(1)}, u32[]{:S(2)}, u32[]{:S(2)}) collective-permute-start(bf16[1,64,1024]{2,1,0:T(8,128)(2,1)S(1)} %get-tuple-element.6), channel_id=1, source_target_pairs={{0,16},{4,20},{8,24},{12,28},{16,0},{20,4},{24,8},{28,12},{1,17},{... | collective-permute-start | bytes 393224 | tf_op jit(solution)/shard_map/ppermute | solution.py:18
  35.8 28.5 %collective-permute-start.4 = (bf16[1,64,1024]{2,1,0:T(8,128)(2,1)S(1)}, bf16[1,64,1024]{2,1,0:T(8,128)(2,1)S(1)}, u32[]{:S(2)}, u32[]{:S(2)}) collective-permute-start(bf16[1,64,1024]{2,1,0:T(8,128)(2,1)S(1)} %get-tuple-element.5), channel_id=1, source_target_pairs={{0,20},{4,16},{8,28},{12,24},{16,4},{20,0},{24,12},{28,8},{1,21},{... | collective-permute-start | bytes 393224 | tf_op jit(solution)/shard_map/ppermute | solution.py:18
  35.9 28.4 %collective-permute-start.5 = (bf16[1,64,1024]{2,1,0:T(8,128)(2,1)S(1)}, bf16[1,64,1024]{2,1,0:T(8,128)(2,1)S(1)}, u32[]{:S(2)}, u32[]{:S(2)}) collective-permute-start(bf16[1,64,1024]{2,1,0:T(8,128)(2,1)S(1)} %get-tuple-element.4), channel_id=1, source_target_pairs={{0,24},{4,28},{8,16},{12,20},{16,8},{20,12},{24,0},{28,4},{1,25},{... | collective-permute-start | bytes 393224 | tf_op jit(solution)/shard_map/ppermute | solution.py:18
  42.5 21.9 %collective-permute-start.6 = (bf16[1,64,1024]{2,1,0:T(8,128)(2,1)S(1)}, bf16[1,64,1024]{2,1,0:T(8,128)(2,1)S(1)}, u32[]{:S(2)}, u32[]{:S(2)}) collective-permute-start(bf16[1,64,1024]{2,1,0:T(8,128)(2,1)S(1)} %get-tuple-element.3), channel_id=1, source_target_pairs={{0,28},{4,24},{8,20},{12,16},{16,12},{20,8},{24,4},{28,0},{1,29},{... | collective-permute-start | bytes 393224 | tf_op jit(solution)/shard_map/ppermute | solution.py:18
  64.4 1.1 copy-start.2
  65.6 0.9 copy-start.3
  66.3 0.9 copy-start.6
  68.7 60.1 %reduce-scatter.6.cloned.1.call-start = ((), (), s32[]{:S(2)}) async-start(), calls=%async_computation.5 | async-start | bytes 983040 | tf_op jit(solution)/shard_map/reduce_scatter | solution.py:82
  68.7 2.8 %copy-start.4 = (f32[512,384]{1,0:T(8,128)S(1)}, f32[512,384]{1,0:T(8,128)}, u32[]{:S(2)}) copy-start(f32[512,384]{1,0:T(8,128)} %copy-done.3) | copy-start | bytes 2359300
  70.7 0.9 copy-start.8
  71.6 1.8 %copy-start.5 = (f32[512,384]{1,0:T(8,128)S(1)}, f32[512,384]{1,0:T(8,128)}, u32[]{:S(2)}) copy-start(f32[512,384]{1,0:T(8,128)} %copy-done.3) | copy-start | bytes 2359300
  71.6 1.8 %copy-start.7 = (f32[512,384]{1,0:T(8,128)S(1)}, f32[512,384]{1,0:T(8,128)}, u32[]{:S(2)}) copy-start(f32[512,384]{1,0:T(8,128)} %copy-done.6) | copy-start | bytes 2359300
  73.3 85.2 %reduce-scatter.4.cloned.1.call-start = ((), (), s32[]{:S(2)}) async-start(), calls=%async_computation.4 | async-start | bytes 983040 | tf_op jit(solution)/shard_map/reduce_scatter | solution.py:79
Sparse Core Ops, SparseCore 0:
  68.8 30.3 reduce-scatter.7
  102.6 26.1 reduce-scatter.5
  132.3 26.1 reduce-scatter.3
